TPU v7x, 32 devices: a whole 2x2x4 slice. The times are simulated.
32 devices in a mesh: batch: 4 (over y, x), dom: 8 (over z, core).
Axes of the slice: x: 2, y: 2, z: 4, core: 2. Of those that a mesh axis runs over, the one named last changes fastest.
Arguments:
- cell_feat: bfloat16 [4, 4096, 256], P('batch', 'dom'), may hold values from -6 to 6
- net_feat: bfloat16 [4, 4096, 256], P('batch', 'dom'), may hold values from -6 to 6
- net_grad: bfloat16 [4, 4096, 256], P('batch', 'dom'), may hold values from -6 to 6
- w_first: bfloat16 [512, 512], replicated, may hold values from -0.25 to 0.25
- w_second: bfloat16 [512, 256], replicated, may hold values from -0.25 to 0.25
- pin_cell: int32 [4, 8, 8, 256], P('batch', 'dom'), may hold values from 0 to 511
- pin_net: int32 [4, 8, 8, 256], P('batch', 'dom'), may hold values from 0 to 511
- pin_count: int32 [4, 8, 8], P('batch', 'dom'), may hold values from 224 to 256, as said below
Outputs:
- cell_out: float32 [4, 4096, 256], P('batch', 'dom')
- net_out: float32 [4, 4096, 256], P('batch', 'dom')
- first_total: float32 [512, 512], replicated
- second_total: float32 [512, 256], replicated
Inputs may be any that keep to these rules, and one draw needn't show every extreme that they name: `pin_count`: every partition sends at most 256 live slots to each owner, and in every design each partition fills its slots to some owner.
All inputs are finite; a program needn't handle non-finite values.
Results may differ from a plain program's by a relative error of at most 0.004.
Values may be sent and summed in bfloat16 or wider, within the bound.
A program may use at most 64 MiB of HBM per device.

v0:
```python
import math
import jax
import jax.numpy as jnp
from jax import lax
from jax.sharding import PartitionSpec as P


def backward_core(pin_input, pin_grad, w_first, w_second):
    pre_act = jnp.dot(pin_input, w_first, preferred_element_type=jnp.float32)
    hidden = jax.nn.silu(pre_act).astype(jnp.bfloat16)
    second_part = lax.dot_general(
        hidden, pin_grad, (((0,), (0,)), ((), ())), preferred_element_type=jnp.float32
    )
    hidden_grad = lax.dot_general(
        pin_grad, w_second, (((1,), (1,)), ((), ())), preferred_element_type=jnp.float32
    )
    gate_sig = jax.nn.sigmoid(pre_act)
    pre_grad = (hidden_grad * gate_sig * (1.0 + pre_act * (1.0 - gate_sig))).astype(jnp.bfloat16)
    first_part = lax.dot_general(
        pin_input, pre_grad, (((0,), (0,)), ((), ())), preferred_element_type=jnp.float32
    )
    input_grad = lax.dot_general(
        pre_grad, w_first, (((1,), (1,)), ((), ())), preferred_element_type=jnp.float32
    ).astype(jnp.bfloat16)
    return (input_grad, first_part, second_part)


def segment_rows(row_index, values, segment_count):
    one_hot = (row_index[:, None] == lax.broadcasted_iota(jnp.int32, (1, segment_count), 1)).astype(
        jnp.bfloat16
    )
    return lax.dot_general(
        one_hot, values, (((0,), (0,)), ((), ())), preferred_element_type=jnp.float32
    )


def on_device(cell_feat, net_feat, net_grad, w_first, w_second, pin_cell, pin_net, pin_count):
    owners = lax.axis_size("dom")
    cell_table = cell_feat[0]
    net_table = net_feat[0]
    grad_table = net_grad[0]
    slot_cell = pin_cell[0, 0]
    slot_net = pin_net[0, 0]
    counts = pin_count[0, 0]
    capacity = slot_cell.shape[1]
    feat_width = cell_table.shape[1]
    is_live = lax.broadcasted_iota(jnp.int32, (owners, capacity), 1) < counts[:, None]
    net_code = jnp.where(is_live, slot_net, -1)
    cell_flat = slot_cell.reshape(-1)
    cell_rows = jnp.take(cell_table, cell_flat, axis=0)
    zero_bf = jnp.zeros((), jnp.bfloat16)
    requested = lax.all_to_all(net_code, "dom", split_axis=0, concat_axis=0, tiled=True)
    code_flat = requested.reshape(-1)
    net_index = jnp.maximum(code_flat, 0)
    net_rows = jnp.take(net_table, net_index, axis=0)
    grad_rows = jnp.where(
        (code_flat >= 0)[:, None], jnp.take(grad_table, net_index, axis=0), zero_bf
    )
    got_rows, got_grads = (
        lax.all_to_all(
            net_rows.reshape(owners, capacity, feat_width),
            "dom",
            split_axis=0,
            concat_axis=0,
            tiled=True,
        ),
        lax.all_to_all(
            grad_rows.reshape(owners, capacity, feat_width),
            "dom",
            split_axis=0,
            concat_axis=0,
            tiled=True,
        ),
    )
    pin_input = jnp.concatenate([cell_rows, got_rows.reshape(-1, feat_width)], axis=1)
    input_grad, first_part, second_part = backward_core(
        pin_input, got_grads.reshape(-1, feat_width), w_first, w_second
    )
    cell_out = segment_rows(cell_flat, input_grad[:, :feat_width], cell_table.shape[0])
    returned = lax.all_to_all(
        input_grad[:, feat_width:].reshape(owners, capacity, feat_width),
        "dom",
        split_axis=0,
        concat_axis=0,
        tiled=True,
    )
    net_out = segment_rows(net_index, returned.reshape(-1, feat_width), net_table.shape[0])
    first_sum, second_sum = lax.psum((first_part, second_part), ("batch", "dom"))
    wgrad_scale = 1.0 / math.sqrt(lax.axis_size("batch") * owners * owners * capacity)
    return (cell_out[None], net_out[None], first_sum * wgrad_scale, second_sum * wgrad_scale)


def solution(mesh):
    return jax.shard_map(
        on_device,
        mesh=mesh,
        in_specs=(
            P("batch", "dom", None),
            P("batch", "dom", None),
            P("batch", "dom", None),
            P(),
            P(),
            P("batch", "dom", None, None),
            P("batch", "dom", None, None),
            P("batch", "dom", None),
        ),
        out_specs=(P("batch", "dom", None), P("batch", "dom", None), P(), P()),
        check_vma=False,
    )
```

profile of v0, /device:TPU:0, one launch (start us, length us, event | category | flops | bytes accessed | tf_op | source)
XLA Modules:
  0.0 270.1 jit_solution(1571650209187003646)
XLA Ops:
  7.2 0.0 copy-start
  7.2 0.8 compare_select_fusion
  8.0 11.7 %all_to_all.21 = s32[8,1,256]{2,1,0:T(1,128)S(1)} all-to-all(s32[8,1,256]{2,1,0:T(1,128)S(1)} %compare_select_fusion), channel_id=1, replica_groups=mesh['batch'=4,'dom'=8] {'dom'}, dimensions={0} | all-to-all | bytes 16384 | tf_op jit(solution)/shard_map/all_to_all | solution.py:52
  19.8 0.0 copy-start.1
  19.9 7.7 %gather_fusion.2 = bf16[2048,256]{1,0:T(8,128)(2,1)S(1)} fusion(bf16[512,256]{1,0:T(8,128)(2,1)} %bitcast.26, s32[2048]{0:T(1024)S(1)} %fusion.10), kind=kCustom, calls=%fused_computation.2.clone | custom fusion | bytes 2105344 | tf_op jit(solution)/shard_map/jit(_take)/gather | solution.py:55
  27.5 7.5 %gather_fusion = bf16[2048,256]{1,0:T(8,128)(2,1)S(1)} fusion(bf16[512,256]{1,0:T(8,128)(2,1)S(1)} %bitcast.27, s32[2048]{0:T(1024)S(1)} %fusion.10), kind=kCustom, calls=%fused_computation.clone | custom fusion | bytes 2105344 | tf_op jit(solution)/shard_map/jit(_take)/gather | solution.py:57
  35.0 0.0 copy-start.4
  35.1 0.0 copy-start.2
  35.1 2.4 select_select_fusion
  37.5 29.7 %all_to_all.22 = bf16[8,256,256]{2,1,0:T(8,128)(2,1)} all-to-all(bf16[8,256,256]{2,1,0:T(8,128)(2,1)S(1)} %bitcast.29), channel_id=1, replica_groups=mesh['batch'=4,'dom'=8] {'dom'}, dimensions={0} | all-to-all | bytes 2097152 | tf_op jit(solution)/shard_map/all_to_all | solution.py:60
  67.2 4.2 %all-to-all-start.1 = ((bf16[8,256,256]{2,1,0:T(8,128)(2,1)}), bf16[8,256,256]{2,1,0:T(8,128)(2,1)}, u32[]{:S(2)}, u32[]{:S(2)}) async-start(bf16[8,256,256]{2,1,0:T(8,128)(2,1)} %bitcast.3), calls=%async_computation.1 | async-start | bytes 2097152 | tf_op jit(solution)/shard_map/all_to_all | solution.py:67
  71.5 0.0 copy-done.4
  71.5 7.5 %gather_fusion.1 = bf16[2048,256]{1,0:T(8,128)(2,1)S(1)} fusion(bf16[512,256]{1,0:T(8,128)(2,1)S(1)} %bitcast.28, s32[2048]{0:T(1024)S(1)} %fusion.11), kind=kCustom, calls=%fused_computation.1.clone | custom fusion | bytes 2105344 | tf_op jit(solution)/shard_map/jit(_take)/gather | solution.py:50
  79.0 0.4 broadcast_select_fusion
  79.5 0.0 copy-done
  79.5 0.0 copy-start.5
  79.5 4.5 %fusion.6 = f32[2048,512]{1,0:T(8,128)} fusion(bf16[512,512]{1,0:T(8,128)(2,1)S(1)} %copy-done, bf16[2048,256]{1,0:T(8,128)(2,1)} %bitcast.31, bf16[2048,256]{1,0:T(8,128)(2,1)S(1)} %broadcast_select_fusion), kind=kOutput, calls=%fused_computation.16 | convolution fusion | flops 1077936128 | bytes 6815744 | tf_op jit(solution)/shard_map/dot_general | solution.py:9
  84.0 14.1 %all-to-all-done.1 = bf16[8,256,256]{2,1,0:T(8,128)(2,1)} async-done(((bf16[8,256,256]{2,1,0:T(8,128)(2,1)}), bf16[8,256,256]{2,1,0:T(8,128)(2,1)}, u32[]{:S(2)}, u32[]{:S(2)}) %all-to-all-start.1) | async-done | bytes 1048608 | tf_op jit(solution)/shard_map/all_to_all | solution.py:67
  98.1 4.2 %multiply_convert_fusion.1 = bf16[2048,512]{1,0:T(8,128)(2,1)S(1)} fusion(f32[2048,512]{1,0:T(8,128)} %fusion.6, bf16[2048,256]{1,0:T(8,128)(2,1)} %bitcast.4, bf16[512,256]{1,0:T(8,128)(2,1)S(1)} %copy-done.5), kind=kOutput, calls=%fused_computation.5 | convolution fusion | flops 546308096 | bytes 7602176 | tf_op jit(solution)/shard_map/dot_general | solution.py:14
  102.3 2.6 convolution_convert_fusion
  104.9 2.3 slice.15
  107.3 3.6 %all-to-all-start.3 = ((bf16[8,256,256]{2,1,0:T(8,128)(2,1)}), bf16[8,256,256]{2,1,0:T(8,128)(2,1)S(1)}, u32[]{:S(2)}, u32[]{:S(2)}) async-start(bf16[8,256,256]{2,1,0:T(8,128)(2,1)} %bitcast.10), calls=%async_computation.3 | async-start | bytes 2097152 | tf_op jit(solution)/shard_map/all_to_all | solution.py:80
  110.8 0.2 all-reduce.3.cloned.1.call-start
  111.1 4.7 %fusion.4 = f32[512,256]{1,0:T(8,128)} fusion(bf16[2048,256]{1,0:T(8,128)(2,1)} %bitcast.4, f32[2048,512]{1,0:T(8,128)} %fusion.6), kind=kOutput, calls=%fused_computation.14 | convolution fusion | flops 542113792 | bytes 5767168 | tf_op jit(solution)/shard_map/dot_general | solution.py:11
  115.8 2.2 fusion.5
  118.0 0.0 all-reduce.3.cloned.1.call-update
  118.1 3.6 %fusion.8 = f32[1,512,256]{2,1,0:T(8,128)} fusion(s32[2048]{0:T(1024)S(1)} %bitcast.38, bf16[2048,512]{1,0:T(8,128)(2,1)} %convolution_convert_fusion), kind=kOutput, calls=%fused_computation.18 | convolution fusion | flops 537919488 | bytes 1581056 | tf_op jit(solution)/shard_map/dot_general | solution.py:32
  121.7 135.0 %all-reduce.3.cloned.1.call-done = (f32[512,512]{1,0:T(8,128)}, f32[512,256]{1,0:T(8,128)}) async-done(((f32[512,512]{1,0:T(8,128)}, f32[512,256]{1,0:T(8,128)}), (f32[512,512]{1,0:T(8,128)}, f32[512,256]{1,0:T(8,128)})) %all-reduce.3.cloned.1.call-update) | async-done | bytes 1572880 | tf_op jit(solution)/shard_map/psum | solution.py:88
  256.7 1.9 broadcast_multiply_fusion.1
  258.6 2.3 broadcast_multiply_fusion
  260.9 0.0 all-to-all-done.3
  260.9 2.4 fusion.7
  (17 shorter events, 0.1 us)
Async XLA Ops:
  7.2 72.3 %copy-start = (bf16[512,512]{1,0:T(8,128)(2,1)S(1)}, bf16[512,512]{1,0:T(8,128)(2,1)}, u32[]{:S(2)}) copy-start(bf16[512,512]{1,0:T(8,128)(2,1)} %param.13) | copy-start | bytes 1572868
  19.8 7.7 %copy-start.1 = (bf16[1,512,256]{2,1,0:T(8,128)(2,1)S(1)}, bf16[1,512,256]{2,1,0:T(8,128)(2,1)}, u32[]{:S(2)}) copy-start(bf16[1,512,256]{2,1,0:T(8,128)(2,1)} %param.12) | copy-start | bytes 786436
  35.0 36.4 %copy-start.4 = (s32[1,1,8,256]{3,2,1,0:T(8,128)S(1)}, s32[1,1,8,256]{3,2,1,0:T(8,128)}, u32[]{:S(2)}) copy-start(s32[1,1,8,256]{3,2,1,0:T(8,128)} %param.15) | copy-start | bytes 24580
  35.1 36.4 %copy-start.2 = (bf16[1,512,256]{2,1,0:T(8,128)(2,1)S(1)}, bf16[1,512,256]{2,1,0:T(8,128)(2,1)}, u32[]{:S(2)}) copy-start(bf16[1,512,256]{2,1,0:T(8,128)(2,1)} %param.10) | copy-start | bytes 786436
  67.2 30.8 %all-to-all-start.1 = ((bf16[8,256,256]{2,1,0:T(8,128)(2,1)}), bf16[8,256,256]{2,1,0:T(8,128)(2,1)}, u32[]{:S(2)}, u32[]{:S(2)}) async-start(bf16[8,256,256]{2,1,0:T(8,128)(2,1)} %bitcast.3), calls=%async_computation.1 | async-start | bytes 2097152 | tf_op jit(solution)/shard_map/all_to_all | solution.py:67
  79.5 18.6 %copy-start.5 = (bf16[512,256]{1,0:T(8,128)(2,1)S(1)}, bf16[512,256]{1,0:T(8,128)(2,1)}, u32[]{:S(2)}) copy-start(bf16[512,256]{1,0:T(8,128)(2,1)} %param.14) | copy-start | bytes 786436
  102.3 2.6 copy-start.6
  107.3 153.6 %all-to-all-start.3 = ((bf16[8,256,256]{2,1,0:T(8,128)(2,1)}), bf16[8,256,256]{2,1,0:T(8,128)(2,1)S(1)}, u32[]{:S(2)}, u32[]{:S(2)}) async-start(bf16[8,256,256]{2,1,0:T(8,128)(2,1)} %bitcast.10), calls=%async_computation.3 | async-start | bytes 2097152 | tf_op jit(solution)/shard_map/all_to_all | solution.py:80
  110.8 145.9 %all-reduce.3.cloned.1.call-start = ((), (), s32[]{:S(2)}) async-start(), calls=%async_computation.4 | async-start | bytes 3145728 | tf_op jit(solution)/shard_map/psum | solution.py:88
  111.1 4.7 %copy-start.3 = (bf16[8,256,256]{2,1,0:T(8,128)(2,1)S(1)}, bf16[8,256,256]{2,1,0:T(8,128)(2,1)}, u32[]{:S(2)}) copy-start(bf16[8,256,256]{2,1,0:T(8,128)(2,1)} %all_to_all.22) | copy-start | bytes 3145732
  111.1 4.7 %copy-start.7 = (bf16[2048,512]{1,0:T(8,128)(2,1)S(1)}, bf16[2048,512]{1,0:T(8,128)(2,1)}, u32[]{:S(2)}) copy-start(bf16[2048,512]{1,0:T(8,128)(2,1)} %copy-done.6) | copy-start | bytes 6291460
Sparse Core Ops, SparseCore 0:
  118.2 138.4 all-reduce.2
where the time goes:
time: 271 us; the launch traced here: 270 us
  waiting for transfers between devices  149 us (55%)
  blocking collectives  41.4 us (15%)
  local copies, waits for them, and re-layouts  25.1 us (9%)
  matrix products  24.3 us (9%)
  between operations  14.2 us (5%)
  starting transfers between devices  8.03 us (3%)
  other arithmetic  7.95 us (3%)
    psum x1, waiting for transfers between devices, on_device(): lax.psum((first_part, second_part), ('batch', 'dom'))  135 us
    all_to_all x1, blocking collectives, on_device(): lax.all_to_all(net_rows.reshape(owners, capacity, feat_width), 'dom', spl...  29.7 us
    all_to_all x1, waiting for transfers between devices, on_device(): lax.all_to_all(grad_rows.reshape(owners, capacity, feat_width), 'dom', sp...  14.1 us
    all_to_all x1, blocking collectives, on_device(): lax.all_to_all(net_code, 'dom', split_axis=0, concat_axis=0, tiled=True)  11.7 us
    gather x1, local copies, waits for them, and re-layouts, on_device(): net_rows = jnp.take(net_table, net_index, axis=0)  7.67 us
    gather x1, local copies, waits for them, and re-layouts, on_device(): jnp.take(grad_table, net_index, axis=0)  7.5 us
    gather x1, local copies, waits for them, and re-layouts, on_device(): cell_rows = jnp.take(cell_table, cell_flat, axis=0)  7.5 us
    dot_general x2, matrix products, segment_rows(): lax.dot_general(one_hot, values, (((0,), (0,)), ((), ())), preferred_elem...  5.99 us
  transfers between devices with their start and end apart: 3, of which 2 were waited for; matrix products, arithmetic and copies ran while one was open for 10% of the time, Pallas kernels for 0%

commit v1 on v0

--- a/solution.py
+++ b/solution.py
@@ -85,7 +85,7 @@
         tiled=True,
     )
     net_out = segment_rows(net_index, returned.reshape(-1, feat_width), net_table.shape[0])
-    first_sum, second_sum = lax.psum((first_part, second_part), ("batch", "dom"))
+    first_sum, second_sum = lax.psum(lax.psum((first_part, second_part), "dom"), "batch")
     wgrad_scale = 1.0 / math.sqrt(lax.axis_size("batch") * owners * owners * capacity)
     return (cell_out[None], net_out[None], first_sum * wgrad_scale, second_sum * wgrad_scale)
 

time: 271 us -> 262 us (0.967)
  waiting for transfers between devices: 149 us -> 140 us
    psum x1 -> x2, waiting for transfers between devices: 135 us -> 125 us  [the longest x1 67.9 us: on_device(): lax.psum((first_part, second_part), 'dom')]
  transfers between devices with their start and end apart: 3 -> 4, of which waited for: 2 -> 3; matrix products, arithmetic and copies ran while one was open for 10% -> 9% of each run, Pallas kernels for 0% -> 0%
where the time goes in v1:
time: 262 us; the launch traced here: 261 us
  waiting for transfers between devices  140 us (53%)
  blocking collectives  41.4 us (16%)
  local copies, waits for them, and re-layouts  26.4 us (10%)
  matrix products  23.4 us (9%)
  between operations  14.2 us (5%)
  starting transfers between devices  8.08 us (3%)
  other arithmetic  7.95 us (3%)
    psum x1, waiting for transfers between devices, on_device(): lax.psum((first_part, second_part), 'dom')  67.9 us
    psum x1, waiting for transfers between devices, on_device(): lax.psum(lax.psum((first_part, second_part), 'dom'), 'batch')  57.5 us
    all_to_all x1, blocking collectives, on_device(): lax.all_to_all(net_rows.reshape(owners, capacity, feat_width), 'dom', spl...  29.7 us
    all_to_all x1, waiting for transfers between devices, on_device(): lax.all_to_all(grad_rows.reshape(owners, capacity, feat_width), 'dom', sp...  14.1 us
    all_to_all x1, blocking collectives, on_device(): lax.all_to_all(net_code, 'dom', split_axis=0, concat_axis=0, tiled=True)  11.7 us
    gather x1, local copies, waits for them, and re-layouts, on_device(): net_rows = jnp.take(net_table, net_index, axis=0)  7.67 us
    gather x1, local copies, waits for them, and re-layouts, on_device(): jnp.take(grad_table, net_index, axis=0)  7.5 us
    gather x1, local copies, waits for them, and re-layouts, on_device(): cell_rows = jnp.take(cell_table, cell_flat, axis=0)  7.5 us
  transfers between devices with their start and end apart: 4, of which 3 were waited for; matrix products, arithmetic and copies ran while one was open for 9% of the time, Pallas kernels for 0%

profile of v1, /device:TPU:0, one launch (start us, length us, event | category | flops | bytes accessed | tf_op | source)
XLA Modules:
  0.0 261.1 jit_solution(17964258669706115366)
XLA Ops:
  7.2 0.0 copy-start
  7.2 0.8 compare_select_fusion
  8.0 11.7 %all_to_all.21 = s32[8,1,256]{2,1,0:T(1,128)S(1)} all-to-all(s32[8,1,256]{2,1,0:T(1,128)S(1)} %compare_select_fusion), channel_id=1, replica_groups=mesh['batch'=4,'dom'=8] {'dom'}, dimensions={0} | all-to-all | bytes 16384 | tf_op jit(solution)/shard_map/all_to_all | solution.py:52
  19.8 0.0 copy-start.1
  19.9 7.7 %gather_fusion.2 = bf16[2048,256]{1,0:T(8,128)(2,1)S(1)} fusion(bf16[512,256]{1,0:T(8,128)(2,1)} %bitcast.26, s32[2048]{0:T(1024)S(1)} %fusion.10), kind=kCustom, calls=%fused_computation.2.clone | custom fusion | bytes 2105344 | tf_op jit(solution)/shard_map/jit(_take)/gather | solution.py:55
  27.5 7.5 %gather_fusion = bf16[2048,256]{1,0:T(8,128)(2,1)S(1)} fusion(bf16[512,256]{1,0:T(8,128)(2,1)S(1)} %bitcast.27, s32[2048]{0:T(1024)S(1)} %fusion.10), kind=kCustom, calls=%fused_computation.clone | custom fusion | bytes 2105344 | tf_op jit(solution)/shard_map/jit(_take)/gather | solution.py:57
  35.0 0.0 copy-start.5
  35.1 2.4 select_select_fusion
  37.5 29.7 %all_to_all.22 = bf16[8,256,256]{2,1,0:T(8,128)(2,1)} all-to-all(bf16[8,256,256]{2,1,0:T(8,128)(2,1)S(1)} %bitcast.29), channel_id=1, replica_groups=mesh['batch'=4,'dom'=8] {'dom'}, dimensions={0} | all-to-all | bytes 2097152 | tf_op jit(solution)/shard_map/all_to_all | solution.py:60
  67.2 4.3 %all-to-all-start.1 = ((bf16[8,256,256]{2,1,0:T(8,128)(2,1)}), bf16[8,256,256]{2,1,0:T(8,128)(2,1)}, u32[]{:S(2)}, u32[]{:S(2)}) async-start(bf16[8,256,256]{2,1,0:T(8,128)(2,1)} %bitcast.3), calls=%async_computation.1 | async-start | bytes 2097152 | tf_op jit(solution)/shard_map/all_to_all | solution.py:67
  71.5 0.0 all-reduce.5.cloned.1.call-start
  71.6 7.5 %gather_fusion.1 = bf16[2048,256]{1,0:T(8,128)(2,1)S(1)} fusion(bf16[512,256]{1,0:T(8,128)(2,1)S(1)} %bitcast.28, s32[2048]{0:T(1024)S(1)} %fusion.11), kind=kCustom, calls=%fused_computation.1.clone | custom fusion | bytes 2105344 | tf_op jit(solution)/shard_map/jit(_take)/gather | solution.py:50
  79.1 0.4 broadcast_select_fusion
  79.6 4.4 %fusion.6 = f32[2048,512]{1,0:T(8,128)} fusion(bf16[512,512]{1,0:T(8,128)(2,1)S(1)} %copy-done, bf16[2048,256]{1,0:T(8,128)(2,1)} %bitcast.31, bf16[2048,256]{1,0:T(8,128)(2,1)S(1)} %broadcast_select_fusion), kind=kOutput, calls=%fused_computation.16 | convolution fusion | flops 1077936128 | bytes 6815744 | tf_op jit(solution)/shard_map/dot_general | solution.py:9
  84.0 14.1 %all-to-all-done.1 = bf16[8,256,256]{2,1,0:T(8,128)(2,1)} async-done(((bf16[8,256,256]{2,1,0:T(8,128)(2,1)}), bf16[8,256,256]{2,1,0:T(8,128)(2,1)}, u32[]{:S(2)}, u32[]{:S(2)}) %all-to-all-start.1) | async-done | bytes 1048608 | tf_op jit(solution)/shard_map/all_to_all | solution.py:67
  98.1 4.7 %fusion.4 = f32[512,256]{1,0:T(8,128)} fusion(bf16[2048,256]{1,0:T(8,128)(2,1)} %bitcast.4, f32[2048,512]{1,0:T(8,128)} %fusion.6), kind=kOutput, calls=%fused_computation.14 | convolution fusion | flops 542113792 | bytes 5767168 | tf_op jit(solution)/shard_map/dot_general | solution.py:11
  102.8 3.1 %multiply_convert_fusion.1 = bf16[2048,512]{1,0:T(8,128)(2,1)S(1)} fusion(f32[2048,512]{1,0:T(8,128)S(1)} %copy-done.7, bf16[2048,256]{1,0:T(8,128)(2,1)} %bitcast.4, bf16[512,256]{1,0:T(8,128)(2,1)S(1)} %copy-done.6), kind=kOutput, calls=%fused_computation.5 | convolution fusion | flops 546308096 | bytes 7602176 | tf_op jit(solution)/shard_map/dot_general | solution.py:14
  105.9 1.3 copy-done.8
  107.2 2.3 fusion.5
  109.5 0.0 all-reduce.5.cloned.1.call-update
  109.5 2.9 %convolution_convert_fusion = bf16[2048,512]{1,0:T(8,128)(2,1)S(1)} fusion(bf16[2048,512]{1,0:T(8,128)(2,1)} %copy-done.8, bf16[512,512]{1,0:T(8,128)(2,1)S(1)} %copy-done), kind=kOutput, calls=%fused_computation.10 | convolution fusion | flops 1074790400 | bytes 4718592 | tf_op jit(solution)/shard_map/dot_general | solution.py:22
  112.4 1.3 copy-done.4
  113.7 1.0 slice.15
  114.8 3.6 %all-to-all-start.3 = ((bf16[8,256,256]{2,1,0:T(8,128)(2,1)}), bf16[8,256,256]{2,1,0:T(8,128)(2,1)S(1)}, u32[]{:S(2)}, u32[]{:S(2)}) async-start(bf16[8,256,256]{2,1,0:T(8,128)(2,1)} %bitcast.10), calls=%async_computation.3 | async-start | bytes 2097152 | tf_op jit(solution)/shard_map/all_to_all | solution.py:80
  118.3 0.2 all-reduce.7.cloned.1.call-start
  118.6 67.9 %all-reduce.5.cloned.1.call-done = (f32[512,512]{1,0:T(8,128)}, f32[512,256]{1,0:T(8,128)}) async-done(((f32[512,512]{1,0:T(8,128)}, f32[512,256]{1,0:T(8,128)}), (f32[512,512]{1,0:T(8,128)}, f32[512,256]{1,0:T(8,128)})) %all-reduce.5.cloned.1.call-update) | async-done | bytes 1572880 | tf_op jit(solution)/shard_map/psum | solution.py:88
  186.5 0.0 all-reduce.7.cloned.1.call-update
  186.5 3.6 %fusion.8 = f32[1,512,256]{2,1,0:T(8,128)} fusion(s32[2048]{0:T(1024)S(1)} %bitcast.38, bf16[2048,512]{1,0:T(8,128)(2,1)} %copy-done.4), kind=kOutput, calls=%fused_computation.18 | convolution fusion | flops 537919488 | bytes 1581056 | tf_op jit(solution)/shard_map/dot_general | solution.py:32
  190.1 2.4 fusion.7
  192.5 57.5 %all-reduce.7.cloned.1.call-done = (f32[512,512]{1,0:T(8,128)}, f32[512,256]{1,0:T(8,128)}) async-done(((f32[512,512]{1,0:T(8,128)}, f32[512,256]{1,0:T(8,128)}), (f32[512,512]{1,0:T(8,128)}, f32[512,256]{1,0:T(8,128)})) %all-reduce.7.cloned.1.call-update) | async-done | bytes 1572880 | tf_op jit(solution)/shard_map/psum | solution.py:88
  250.1 2.3 broadcast_multiply_fusion
  252.4 1.9 broadcast_multiply_fusion.1
  (22 shorter events, 0.1 us)
Async XLA Ops:
  7.2 72.4 %copy-start = (bf16[512,512]{1,0:T(8,128)(2,1)S(1)}, bf16[512,512]{1,0:T(8,128)(2,1)}, u32[]{:S(2)}) copy-start(bf16[512,512]{1,0:T(8,128)(2,1)} %param.13) | copy-start | bytes 1572868
  19.8 7.7 %copy-start.1 = (bf16[1,512,256]{2,1,0:T(8,128)(2,1)S(1)}, bf16[1,512,256]{2,1,0:T(8,128)(2,1)}, u32[]{:S(2)}) copy-start(bf16[1,512,256]{2,1,0:T(8,128)(2,1)} %param.12) | copy-start | bytes 786436
  35.0 36.5 %copy-start.5 = (s32[1,1,8,256]{3,2,1,0:T(8,128)S(1)}, s32[1,1,8,256]{3,2,1,0:T(8,128)}, u32[]{:S(2)}) copy-start(s32[1,1,8,256]{3,2,1,0:T(8,128)} %param.15) | copy-start | bytes 24580
  35.1 36.5 %copy-start.2 = (bf16[1,512,256]{2,1,0:T(8,128)(2,1)S(1)}, bf16[1,512,256]{2,1,0:T(8,128)(2,1)}, u32[]{:S(2)}) copy-start(bf16[1,512,256]{2,1,0:T(8,128)(2,1)} %param.10) | copy-start | bytes 786436
  67.2 30.9 %all-to-all-start.1 = ((bf16[8,256,256]{2,1,0:T(8,128)(2,1)}), bf16[8,256,256]{2,1,0:T(8,128)(2,1)}, u32[]{:S(2)}, u32[]{:S(2)}) async-start(bf16[8,256,256]{2,1,0:T(8,128)(2,1)} %bitcast.3), calls=%async_computation.1 | async-start | bytes 2097152 | tf_op jit(solution)/shard_map/all_to_all | solution.py:67
  71.5 115.0 %all-reduce.5.cloned.1.call-start = ((), (), s32[]{:S(2)}) async-start(), calls=%async_computation.4 | async-start | bytes 3145728 | tf_op jit(solution)/shard_map/psum | solution.py:88
  98.1 4.7 %copy-start.6 = (bf16[512,256]{1,0:T(8,128)(2,1)S(1)}, bf16[512,256]{1,0:T(8,128)(2,1)}, u32[]{:S(2)}) copy-start(bf16[512,256]{1,0:T(8,128)(2,1)} %param.14) | copy-start | bytes 786436
  98.1 4.7 %copy-start.7 = (f32[2048,512]{1,0:T(8,128)S(1)}, f32[2048,512]{1,0:T(8,128)}, u32[]{:S(2)}) copy-start(f32[2048,512]{1,0:T(8,128)} %fusion.6) | copy-start | bytes 12582916
  102.8 4.4 %copy-start.3 = (bf16[8,256,256]{2,1,0:T(8,128)(2,1)S(1)}, bf16[8,256,256]{2,1,0:T(8,128)(2,1)}, u32[]{:S(2)}) copy-start(bf16[8,256,256]{2,1,0:T(8,128)(2,1)} %all_to_all.22) | copy-start | bytes 3145732
  105.9 1.3 copy-start.8
  112.4 1.3 copy-start.4
  114.8 75.4 %all-to-all-start.3 = ((bf16[8,256,256]{2,1,0:T(8,128)(2,1)}), bf16[8,256,256]{2,1,0:T(8,128)(2,1)S(1)}, u32[]{:S(2)}, u32[]{:S(2)}) async-start(bf16[8,256,256]{2,1,0:T(8,128)(2,1)} %bitcast.10), calls=%async_computation.3 | async-start | bytes 2097152 | tf_op jit(solution)/shard_map/all_to_all | solution.py:80
  118.3 131.7 %all-reduce.7.cloned.1.call-start = ((), (), s32[]{:S(2)}) async-start(), calls=%async_computation.5 | async-start | bytes 3145728 | tf_op jit(solution)/shard_map/psum | solution.py:88
Sparse Core Ops, SparseCore 0:
  109.6 76.8 all-reduce.4
  189.6 60.3 all-reduce.6
